TPU v7x, 512 devices: a whole 4x8x8 slice. The times are simulated.
512 devices in a mesh: gx: 8 (over z), gy: 8 (over y_lo, core), gz: 8 (over y_hi, x).
Axes of the slice: x: 4, y: 8 (y_hi: 2, y_lo: 4; y = y_hi * 4 + y_lo), z: 8, core: 2. Of those that a mesh axis runs over, the one named last changes fastest.
Arguments:
- x_in: bfloat16 [3072, 5120], P(('gy', 'gx'), 'gz'), may hold values from -190 to 190
- gain: float32 [5120], P('gz'), may hold values from 0.25 to 1.75
- w_up: bfloat16 [5120, 7168], P(('gz', 'gy'), 'gx'), may hold values from -0.078125 to 0.078125
- w_down: bfloat16 [7168, 5120], P(('gx', 'gy'), 'gz'), may hold values from -0.0625 to 0.0625
- d_out: bfloat16 [3072, 5120], P(('gy', 'gx'), 'gz'), may hold values from -1.1953125 to 1.1953125
Outputs:
- d_x: bfloat16 [3072, 5120], P(('gy', 'gx'), 'gz')
- d_w_up: bfloat16 [5120, 7168], P(('gz', 'gy'), 'gx')
- d_w_down: bfloat16 [7168, 5120], P(('gx', 'gy'), 'gz')
- d_gain: float32 [5120], P('gz')
All inputs are finite; a program needn't handle non-finite values.
Results may differ from a plain program's by a relative error of at most 0.02.
Values may be sent and summed in bfloat16 or wider, within the bound.
No kernel may reach another device: no remote copies, remote signals or barrier semaphores. Data moves between devices by JAX's collectives and lax.ppermute only.
A program may use at most 64 MiB of HBM per device.

v0:
```python
import jax
import jax.numpy as jnp
from jax import lax
from jax.sharding import PartitionSpec as P


def gelu_pair(hidden):
    cdf = 0.5 * (1.0 + jax.scipy.special.erf(hidden * 0.7071067811865476))
    slope = cdf + hidden * jnp.exp(-0.5 * hidden * hidden) * 0.3989422804014327
    return (hidden * cdf, slope)


def body(x_in, gain, w_up, w_down, d_out):
    width = x_in.shape[1] * lax.axis_size("gz")
    xf = x_in.astype(jnp.float32)
    total = lax.psum(jnp.sum(xf, axis=1), "gz")
    mean = total / width
    centered = xf - mean[:, None]
    var = lax.psum(jnp.sum(centered * centered, axis=1), "gz") / width
    inv = lax.rsqrt(var + 1e-05)[:, None]
    normed = centered * inv
    z_local = (normed * gain).astype(jnp.bfloat16)
    up_full = lax.all_gather(w_up, "gy", axis=0, tiled=True)
    z_rows = lax.all_gather(z_local, "gx", axis=0, tiled=True)
    part_rows = z_rows
    hidden = lax.psum_scatter(
        jnp.dot(part_rows, up_full, preferred_element_type=jnp.float32).astype(jnp.bfloat16),
        "gz",
        scatter_dimension=0,
        tiled=True,
    ).astype(jnp.float32)
    act_f, slope = gelu_pair(hidden)
    act = act_f.astype(jnp.bfloat16)
    down_full = lax.all_gather(w_down, "gy", axis=0, tiled=True)
    out_rows = lax.all_gather(d_out, "gx", axis=0, tiled=True)
    act_rows = lax.all_gather(act, "gz", axis=0, tiled=True)
    part_rows = out_rows
    d_act = lax.psum_scatter(
        lax.dot_general(
            part_rows, down_full, (((1,), (1,)), ((), ())), preferred_element_type=jnp.float32
        ).astype(jnp.bfloat16),
        "gz",
        scatter_dimension=0,
        tiled=True,
    ).astype(jnp.float32)
    d_hidden = (d_act * slope).astype(jnp.bfloat16)
    hgrad_rows = lax.all_gather(d_hidden, "gz", axis=0, tiled=True)
    columns = act_rows
    d_w_down = lax.psum_scatter(
        lax.dot_general(
            columns, out_rows, (((0,), (0,)), ((), ())), preferred_element_type=jnp.float32
        ).astype(jnp.bfloat16),
        "gy",
        scatter_dimension=0,
        tiled=True,
    )
    columns = z_rows
    d_w_up = lax.psum_scatter(
        lax.dot_general(
            columns, hgrad_rows, (((0,), (0,)), ((), ())), preferred_element_type=jnp.float32
        ).astype(jnp.bfloat16),
        "gy",
        scatter_dimension=0,
        tiled=True,
    )
    part_rows = hgrad_rows
    d_z = lax.psum_scatter(
        lax.dot_general(
            part_rows, up_full, (((1,), (1,)), ((), ())), preferred_element_type=jnp.float32
        ).astype(jnp.bfloat16),
        "gx",
        scatter_dimension=0,
        tiled=True,
    ).astype(jnp.float32)
    d_gain = lax.psum(jnp.sum(d_z * normed, axis=0), ("gx", "gy"))
    d_scaled = d_z * gain
    scaled_sum, cross_sum = lax.psum(
        (jnp.sum(d_scaled, axis=1), jnp.sum(d_scaled * normed, axis=1)), "gz"
    )
    d_x = inv * (d_scaled - scaled_sum[:, None] / width - normed * (cross_sum[:, None] / width))
    return (d_x.astype(jnp.bfloat16), d_w_up, d_w_down, d_gain)


def solution(mesh):
    placed = (
        P(("gy", "gx"), "gz"),
        P("gz"),
        P(("gz", "gy"), "gx"),
        P(("gx", "gy"), "gz"),
        P(("gy", "gx"), "gz"),
    )
    return jax.shard_map(
        body,
        mesh=mesh,
        in_specs=placed,
        out_specs=(P(("gy", "gx"), "gz"), P(("gz", "gy"), "gx"), P(("gx", "gy"), "gz"), P("gz")),
        check_vma=False,
    )
```

profile of v0, /device:TPU:1, one launch (start us, length us, event | category | flops | bytes accessed | tf_op | source)
XLA Modules:
  0.0 543.6 jit_solution(16610349977316155122)
XLA Ops:
  7.2 0.0 all-gather.3.cloned.1.call-start
  7.2 0.7 all-gather.3.cloned.1.call-update
  7.9 0.0 all-gather.5.cloned.1.call-start
  7.9 0.7 all-gather.5.cloned.1.call-update
  8.6 0.0 reduce-scatter.6.cloned.1.call-start
  8.7 27.0 %all_gather.18 = bf16[384,640]{1,0:T(8,128)(2,1)S(1)} all-gather(bf16[48,640]{1,0:T(8,128)(2,1)} %param.9), channel_id=1, replica_groups=mesh['gx'=8,'gy'=8,'gz'=8] {'gx'}, dimensions={0}, use_global_device_ids=true | all-gather | bytes 552960 | tf_op jit(solution)/shard_map/all_gather | solution.py:35
  35.7 0.0 copy-start
  35.7 0.0 copy-start.1
  35.7 17.8 %all-gather.3.cloned.1.call-done = bf16[896,640]{1,0:T(8,128)(2,1)} async-done(((bf16[112,640]{1,0:T(8,128)(2,1)}), bf16[896,640]{1,0:T(8,128)(2,1)}) %all-gather.3.cloned.1.call-update) | async-done | bytes 1146896 | tf_op jit(solution)/shard_map/all_gather | solution.py:34
  53.5 2.9 convolution_convert_fusion.3
  56.4 0.0 reduce-scatter.6.cloned.1.call-update
  56.4 0.0 reduce-scatter.8.cloned.1.call-start
  56.5 0.0 copy-done
  56.5 0.1 convert_reduce_fusion
  56.6 26.6 %psum.35 = f32[48]{0:T(128)S(1)} all-reduce(f32[48]{0:T(128)S(1)} %convert_reduce_fusion), channel_id=1, replica_groups=mesh['gx'=8,'gy'=8,'gz'=8] {'gz'}, use_global_device_ids=true, to_apply=%region_1.0 | all-reduce | flops 48 | bytes 384 | tf_op jit(solution)/shard_map/psum | solution.py:16
  83.2 0.2 fusion.20
  83.4 20.3 %psum.36 = f32[48]{0:T(128)S(1)} all-reduce(f32[48]{0:T(128)S(1)} %fusion.20), channel_id=1, replica_groups=mesh['gx'=8,'gy'=8,'gz'=8] {'gz'}, use_global_device_ids=true, to_apply=%region_3.0 | all-reduce | flops 48 | bytes 384 | tf_op jit(solution)/shard_map/psum | solution.py:19
  103.7 0.0 copy-done.1
  103.7 0.1 fusion.16
  103.8 22.4 %all_gather.20 = bf16[384,640]{1,0:T(8,128)(2,1)S(1)} all-gather(bf16[48,640]{1,0:T(8,128)(2,1)S(1)} %fusion.16), channel_id=1, replica_groups=mesh['gx'=8,'gy'=8,'gz'=8] {'gx'}, dimensions={0}, use_global_device_ids=true | all-gather | bytes 552960 | tf_op jit(solution)/shard_map/all_gather | solution.py:24
  126.3 0.0 all-gather.5.cloned.1.call-done
  126.3 2.9 convolution_convert_fusion.2
  129.2 0.0 copy-start.2
  129.2 0.0 reduce-scatter.8.cloned.1.call-update
  129.2 0.0 reduce-scatter.10.cloned.1.call-start
  129.3 56.7 %reduce-scatter.6.cloned.1.call-done = bf16[48,896]{1,0:T(8,128)(2,1)} async-done(((bf16[384,896]{1,0:T(8,128)(2,1)}), bf16[48,896]{1,0:T(8,128)(2,1)}) %reduce-scatter.6.cloned.1.call-update) | async-done | bytes 86032 | tf_op jit(solution)/shard_map/reduce_scatter | solution.py:38
  185.9 88.3 %reduce-scatter.8.cloned.1.call-done = bf16[48,896]{1,0:T(8,128)(2,1)} async-done(((bf16[384,896]{1,0:T(8,128)(2,1)}), bf16[48,896]{1,0:T(8,128)(2,1)}) %reduce-scatter.8.cloned.1.call-update) | async-done | bytes 86032 | tf_op jit(solution)/shard_map/reduce_scatter | solution.py:26
  274.3 1.0 fusion.8
  275.3 39.4 %all_gather.22 = bf16[384,896]{1,0:T(8,128)(2,1)S(1)} all-gather(bf16[48,896]{1,0:T(8,128)(2,1)S(1)} %get-tuple-element.10), channel_id=1, replica_groups=mesh['gx'=8,'gy'=8,'gz'=8] {'gz'}, dimensions={0}, use_global_device_ids=true | all-gather | bytes 774144 | tf_op jit(solution)/shard_map/all_gather | solution.py:47
  314.7 0.0 copy-done.2
  314.7 1.6 convolution_convert_fusion.4
  316.3 0.0 reduce-scatter.10.cloned.1.call-update
  316.3 0.0 reduce-scatter.14.cloned.1.call-start
  316.4 41.4 %all_gather.23 = bf16[384,896]{1,0:T(8,128)(2,1)S(1)} all-gather(bf16[48,896]{1,0:T(8,128)(2,1)S(1)} %get-tuple-element.9), channel_id=1, replica_groups=mesh['gx'=8,'gy'=8,'gz'=8] {'gz'}, dimensions={0}, use_global_device_ids=true | all-gather | bytes 774144 | tf_op jit(solution)/shard_map/all_gather | solution.py:36
  357.8 1.9 convolution_convert_fusion
  359.7 0.0 reduce-scatter.14.cloned.1.call-update
  359.7 0.0 reduce-scatter.12.cloned.1.call-start
  359.8 1.9 convolution_convert_fusion.1
  361.6 0.0 reduce-scatter.12.cloned.1.call-update
  361.6 0.0 reduce-scatter.10.cloned.1.call-done
  361.7 1.0 fusion.22
  362.7 23.1 %all-reduce = (f32[48]{0:T(128)S(1)}, f32[48]{0:T(128)S(1)}) all-reduce(f32[48]{0:T(128)S(1)} %get-tuple-element.5, f32[48]{0:T(128)S(1)} %get-tuple-element.6), channel_id=1, replica_groups=mesh['gx'=8,'gy'=8,'gz'=8] {'gz'}, use_global_device_ids=true, to_apply=%region_10.0 | all-reduce | flops 96 | bytes 768 | tf_op jit(solution)/shard_map/psum | solution.py:77
  385.9 149.4 %psum.39 = f32[640]{0:T(1024)} all-reduce(f32[640]{0:T(1024)S(1)} %get-tuple-element.4), channel_id=1, replica_groups=mesh['gx'=8,'gy'=8,'gz'=8] {'gx','gy'}, use_global_device_ids=true, to_apply=%region_14.0 | all-reduce | flops 640 | bytes 5120 | tf_op jit(solution)/shard_map/psum | solution.py:75
  535.2 1.6 fusion.19
  536.8 0.0 reduce-scatter.14.cloned.1.call-done
  536.8 0.0 reduce-scatter.12.cloned.1.call-done
  (3 shorter events, 0.0 us)
Async XLA Ops:
  7.2 46.4 %all-gather.3.cloned.1.call-start = ((), (), s32[]{:S(2)}) async-start(), calls=%async_computation.5 | async-start | bytes 1290240 | tf_op jit(solution)/shard_map/all_gather | solution.py:34
  7.9 118.4 %all-gather.5.cloned.1.call-start = ((), (), s32[]{:S(2)}) async-start(), calls=%async_computation.7 | async-start | bytes 1290240 | tf_op jit(solution)/shard_map/all_gather | solution.py:23
  8.6 177.3 %reduce-scatter.6.cloned.1.call-start = ((), (), s32[]{:S(2)}) async-start(), calls=%async_computation.6 | async-start | bytes 774144 | tf_op jit(solution)/shard_map/reduce_scatter | solution.py:38
  35.7 20.8 %copy-start = (bf16[48,640]{1,0:T(8,128)(2,1)S(1)}, bf16[48,640]{1,0:T(8,128)(2,1)}, u32[]{:S(2)}) copy-start(bf16[48,640]{1,0:T(8,128)(2,1)} %param.5) | copy-start | bytes 184324
  35.7 68.0 %copy-start.1 = (f32[640]{0:T(1024)S(1)}, f32[640]{0:T(1024)}, u32[]{:S(2)}) copy-start(f32[640]{0:T(1024)} %param.6) | copy-start | bytes 7684
  56.4 217.8 %reduce-scatter.8.cloned.1.call-start = ((), (), s32[]{:S(2)}) async-start(), calls=%async_computation.8 | async-start | bytes 774144 | tf_op jit(solution)/shard_map/reduce_scatter | solution.py:26
  129.2 185.5 %copy-start.2 = (bf16[640,896]{1,0:T(8,128)(2,1)S(1)}, bf16[640,896]{1,0:T(8,128)(2,1)}, u32[]{:S(2)}) copy-start(bf16[640,896]{1,0:T(8,128)(2,1)} %all-gather.5.cloned.1.call-done) | copy-start | bytes 3440644
  129.2 232.5 %reduce-scatter.10.cloned.1.call-start = ((), (), s32[]{:S(2)}) async-start(), calls=%async_computation.9 | async-start | bytes 552960 | tf_op jit(solution)/shard_map/reduce_scatter | solution.py:67
  316.3 220.5 %reduce-scatter.14.cloned.1.call-start = ((), (), s32[]{:S(2)}) async-start(), calls=%async_computation.11 | async-start | bytes 1290240 | tf_op jit(solution)/shard_map/reduce_scatter | solution.py:49
  359.7 177.1 %reduce-scatter.12.cloned.1.call-start = ((), (), s32[]{:S(2)}) async-start(), calls=%async_computation.10 | async-start | bytes 1290240 | tf_op jit(solution)/shard_map/reduce_scatter | solution.py:58
Sparse Core Ops, SparseCore 0:
  10.1 43.4 all-gather.2
  55.6 39.0 all-gather.4
  99.2 86.6 reduce-scatter.5
  191.0 83.2 reduce-scatter.7
  316.5 40.0 reduce-scatter.9
  360.0 47.1 reduce-scatter.13
  410.9 39.1 reduce-scatter.11
where the time goes:
time: 544 us
  blocking collectives  350 us (64%)
  waiting for transfers between devices  164 us (30%)
  between operations  14.2 us (3%)
  matrix products  11.1 us (2%)
    psum x1, blocking collectives, body(): d_gain = lax.psum(jnp.sum(d_z * normed, axis=0), ('gx', 'gy'))  149 us
    reduce_scatter x1, waiting for transfers between devices, body(): lax.psum_scatter(jnp.dot(part_rows, up_full, preferred_element_type=jnp.f...  88.3 us
    reduce_scatter x1, waiting for transfers between devices, body(): lax.psum_scatter(lax.dot_general(part_rows, down_full, (((1,), (1,)), (()...  56.7 us
    all_gather x1, blocking collectives, body(): act_rows = lax.all_gather(act, 'gz', axis=0, tiled=True)  41.4 us
    all_gather x1, blocking collectives, body(): hgrad_rows = lax.all_gather(d_hidden, 'gz', axis=0, tiled=True)  39.4 us
    all_gather x1, blocking collectives, body(): out_rows = lax.all_gather(d_out, 'gx', axis=0, tiled=True)  27 us
    psum x1, blocking collectives, body(): total = lax.psum(jnp.sum(xf, axis=1), 'gz')  26.6 us
    psum x1, blocking collectives, body(): lax.psum((jnp.sum(d_scaled, axis=1), jnp.sum(d_scaled * normed, axis=1)),...  23.1 us
  transfers between devices with their start and end apart: 7, of which 3 were waited for; matrix products, arithmetic and copies ran while one was open for 2% of the time, Pallas kernels for 0%

commit v1 on v0

--- a/solution.py
+++ b/solution.py
@@ -33,7 +33,6 @@
     act = act_f.astype(jnp.bfloat16)
     down_full = lax.all_gather(w_down, "gy", axis=0, tiled=True)
     out_rows = lax.all_gather(d_out, "gx", axis=0, tiled=True)
-    act_rows = lax.all_gather(act, "gz", axis=0, tiled=True)
     part_rows = out_rows
     d_act = lax.psum_scatter(
         lax.dot_general(
@@ -44,7 +43,16 @@
         tiled=True,
     ).astype(jnp.float32)
     d_hidden = (d_act * slope).astype(jnp.bfloat16)
-    hgrad_rows = lax.all_gather(d_hidden, "gz", axis=0, tiled=True)
+
+    def mix_the_surface(my_data, inp):
+        local_out = jnp.split(
+            lax.all_gather(jnp.concatenate([inp, my_data], 1), "gz", axis=0, tiled=True),
+            [inp.shape[1]],
+            1,
+        )
+        return local_out
+
+    act_rows, hgrad_rows = mix_the_surface(d_hidden, act)
     columns = act_rows
     d_w_down = lax.psum_scatter(
         lax.dot_general(

time: 544 us -> 562 us (1.033)
  waiting for transfers between devices: 164 us -> 262 us
  blocking collectives: 350 us -> 266 us
    all_gather x2 -> x0, blocking collectives: 80.8 us -> none  [the longest x1 41.4 us: body(): act_rows = lax.all_gather(act, 'gz', axis=0, tiled=True)]
    all_gather x0 -> x1, waiting for transfers between devices: none -> 67.5 us  [mix_the_surface(): lax.all_gather(jnp.concatenate([inp, my_data], 1), 'gz', axis=0, tiled=True)]
    reduce_scatter x1, waiting for transfers between devices: 56.7 us -> 88.4 us  [body(): lax.psum_scatter(lax.dot_general(part_rows, down_full, (((1,), (1,)), (()...]
    reduce_scatter x1, waiting for transfers between devices: 0.02 us -> 31.2 us  [body(): lax.psum_scatter(lax.dot_general(part_rows, up_full, (((1,), (1,)), ((),...]
    all_gather x1, waiting for transfers between devices: 17.8 us -> 0.01 us  [body(): down_full = lax.all_gather(w_down, 'gy', axis=0, tiled=True)]
    reduce_scatter x1, waiting for transfers between devices: 88.3 us -> 73.1 us  [body(): lax.psum_scatter(jnp.dot(part_rows, up_full, preferred_element_type=jnp.f...]
    all_gather x1, blocking collectives: 27 us -> 19.4 us  [body(): out_rows = lax.all_gather(d_out, 'gx', axis=0, tiled=True)]
    psum x1, blocking collectives: 149 us -> 143 us  [body(): d_gain = lax.psum(jnp.sum(d_z * normed, axis=0), ('gx', 'gy'))]
  transfers between devices with their start and end apart: 7 -> 8, of which waited for: 3 -> 4; matrix products, arithmetic and copies ran while one was open for 2% -> 3% of each run, Pallas kernels for 0% -> 0%
where the time goes in v1:
time: 562 us; the launch traced here: 561 us
  blocking collectives  266 us (47%)
  waiting for transfers between devices  262 us (47%)
  between operations  14.2 us (3%)
  matrix products  12.3 us (2%)
  other arithmetic  7.2 us (1%)
    psum x1, blocking collectives, body(): d_gain = lax.psum(jnp.sum(d_z * normed, axis=0), ('gx', 'gy'))  143 us
    reduce_scatter x1, waiting for transfers between devices, body(): lax.psum_scatter(lax.dot_general(part_rows, down_full, (((1,), (1,)), (()...  88.4 us
    reduce_scatter x1, waiting for transfers between devices, body(): lax.psum_scatter(jnp.dot(part_rows, up_full, preferred_element_type=jnp.f...  73.1 us
    all_gather x1, waiting for transfers between devices, mix_the_surface(): lax.all_gather(jnp.concatenate([inp, my_data], 1), 'gz', axis=0, tiled=True)  67.5 us
    reduce_scatter x1, waiting for transfers between devices, body(): lax.psum_scatter(lax.dot_general(part_rows, up_full, (((1,), (1,)), ((),...  31.2 us
    psum x1, blocking collectives, body(): total = lax.psum(jnp.sum(xf, axis=1), 'gz')  29 us
    psum x1, blocking collectives, body(): lax.psum((jnp.sum(d_scaled, axis=1), jnp.sum(d_scaled * normed, axis=1)),...  27.7 us
    all_gather x1, blocking collectives, body(): z_rows = lax.all_gather(z_local, 'gx', axis=0, tiled=True)  26.6 us
  transfers between devices with their start and end apart: 8, of which 4 were waited for; matrix products, arithmetic and copies ran while one was open for 3% of the time, Pallas kernels for 0%

profile of v1, /device:TPU:1, one launch (start us, length us, event | category | flops | bytes accessed | tf_op | source)
XLA Modules:
  0.0 561.5 jit_solution(7194614212154251674)
XLA Ops:
  7.2 0.0 all-gather.4.cloned.1.call-start
  7.2 0.7 all-gather.4.cloned.1.call-update
  7.9 0.0 all-gather.6.cloned.1.call-start
  7.9 0.7 all-gather.6.cloned.1.call-update
  8.6 0.0 reduce-scatter.6.cloned.1.call-start
  8.7 0.9 convert_reduce_fusion
  9.6 29.0 %psum.35 = f32[48]{0:T(128)S(1)} all-reduce(f32[48]{0:T(128)S(1)} %convert_reduce_fusion), channel_id=1, replica_groups=mesh['gx'=8,'gy'=8,'gz'=8] {'gz'}, use_global_device_ids=true, to_apply=%region_1.0 | all-reduce | flops 48 | bytes 384 | tf_op jit(solution)/shard_map/psum | solution.py:16
  38.6 1.0 fusion.23
  39.6 20.3 %psum.36 = f32[48]{0:T(128)S(1)} all-reduce(f32[48]{0:T(128)S(1)} %fusion.23), channel_id=1, replica_groups=mesh['gx'=8,'gy'=8,'gz'=8] {'gz'}, use_global_device_ids=true, to_apply=%region_3.0 | all-reduce | flops 48 | bytes 384 | tf_op jit(solution)/shard_map/psum | solution.py:19
  59.9 0.9 fusion.19
  60.9 26.6 %all_gather.15 = bf16[384,640]{1,0:T(8,128)(2,1)S(1)} all-gather(bf16[48,640]{1,0:T(8,128)(2,1)S(1)} %fusion.19), channel_id=1, replica_groups=mesh['gx'=8,'gy'=8,'gz'=8] {'gx'}, dimensions={0}, use_global_device_ids=true | all-gather | bytes 552960 | tf_op jit(solution)/shard_map/all_gather | solution.py:24
  87.5 0.0 copy-start.1
  87.5 0.0 all-gather.4.cloned.1.call-done
  87.5 2.9 convolution_convert_fusion.3
  90.4 0.0 reduce-scatter.6.cloned.1.call-update
  90.4 0.0 reduce-scatter.8.cloned.1.call-start
  90.5 0.0 copy-done.1
  90.5 19.4 %all_gather.17 = bf16[384,640]{1,0:T(8,128)(2,1)S(1)} all-gather(bf16[48,640]{1,0:T(8,128)(2,1)S(1)} %copy-done.1), channel_id=1, replica_groups=mesh['gx'=8,'gy'=8,'gz'=8] {'gx'}, dimensions={0}, use_global_device_ids=true | all-gather | bytes 552960 | tf_op jit(solution)/shard_map/all_gather | solution.py:35
  109.8 0.0 all-gather.6.cloned.1.call-done
  109.8 2.9 convolution_convert_fusion.2
  112.7 0.0 copy-start.4
  112.7 0.0 reduce-scatter.8.cloned.1.call-update
  112.8 0.0 all-gather.8.cloned.1.call-start
  112.8 73.1 %reduce-scatter.6.cloned.1.call-done = bf16[48,896]{1,0:T(8,128)(2,1)} async-done(((bf16[384,896]{1,0:T(8,128)(2,1)}), bf16[48,896]{1,0:T(8,128)(2,1)}) %reduce-scatter.6.cloned.1.call-update) | async-done | bytes 86032 | tf_op jit(solution)/shard_map/reduce_scatter | solution.py:26
  186.0 88.4 %reduce-scatter.8.cloned.1.call-done = bf16[48,896]{1,0:T(8,128)(2,1)} async-done(((bf16[384,896]{1,0:T(8,128)(2,1)}), bf16[48,896]{1,0:T(8,128)(2,1)}) %reduce-scatter.8.cloned.1.call-update) | async-done | bytes 86032 | tf_op jit(solution)/shard_map/reduce_scatter | solution.py:37
  274.4 1.0 fusion.6
  275.4 0.7 pad_maximum_fusion
  276.1 0.0 all-gather.8.cloned.1.call-update
  276.1 0.0 reduce-scatter.10.cloned.1.call-start
  276.1 67.5 %all-gather.8.cloned.1.call-done = bf16[384,1792]{1,0:T(8,128)(2,1)} async-done(((bf16[48,1792]{1,0:T(8,128)(2,1)}), bf16[384,1792]{1,0:T(8,128)(2,1)}) %all-gather.8.cloned.1.call-update) | async-done | bytes 1376272 | tf_op jit(solution)/shard_map/all_gather | solution.py:49
  343.7 0.0 copy-done.4
  343.7 0.0 copy-start.3
  343.7 2.8 convolution_convert_fusion.4
  346.5 0.0 reduce-scatter.10.cloned.1.call-update
  346.5 0.0 reduce-scatter.12.cloned.1.call-start
  346.6 0.0 copy-done.3
  346.6 1.9 convolution_convert_fusion.1
  348.4 0.0 reduce-scatter.12.cloned.1.call-update
  348.5 0.0 reduce-scatter.14.cloned.1.call-start
  348.5 1.9 convolution_convert_fusion
  350.4 0.0 copy-start
  350.4 0.0 copy-start.2
  350.4 0.0 reduce-scatter.14.cloned.1.call-update
  350.4 31.2 %reduce-scatter.10.cloned.1.call-done = bf16[48,640]{1,0:T(8,128)(2,1)} async-done(((bf16[384,640]{1,0:T(8,128)(2,1)}), bf16[48,640]{1,0:T(8,128)(2,1)}) %reduce-scatter.10.cloned.1.call-update) | async-done | bytes 61456 | tf_op jit(solution)/shard_map/reduce_scatter | solution.py:75
  381.6 0.0 copy-done
  381.6 0.0 copy-done.2
  381.6 1.0 fusion.25
  382.6 27.7 %all-reduce = (f32[48]{0:T(128)S(1)}, f32[48]{0:T(128)S(1)}) all-reduce(f32[48]{0:T(128)S(1)} %get-tuple-element.5, f32[48]{0:T(128)S(1)} %get-tuple-element.6), channel_id=1, replica_groups=mesh['gx'=8,'gy'=8,'gz'=8] {'gz'}, use_global_device_ids=true, to_apply=%region_10.0 | all-reduce | flops 96 | bytes 768 | tf_op jit(solution)/shard_map/psum | solution.py:85
  410.3 142.7 %psum.39 = f32[640]{0:T(1024)} all-reduce(f32[640]{0:T(1024)S(1)} %get-tuple-element.4), channel_id=1, replica_groups=mesh['gx'=8,'gy'=8,'gz'=8] {'gx','gy'}, use_global_device_ids=true, to_apply=%region_14.0 | all-reduce | flops 640 | bytes 5120 | tf_op jit(solution)/shard_map/psum | solution.py:83
  553.1 1.6 fusion.22
  554.6 0.0 reduce-scatter.12.cloned.1.call-done
  554.6 0.0 reduce-scatter.14.cloned.1.call-done
  (3 shorter events, 0.0 us)
Async XLA Ops:
  7.2 80.3 %all-gather.4.cloned.1.call-start = ((), (), s32[]{:S(2)}) async-start(), calls=%async_computation.5 | async-start | bytes 1290240 | tf_op jit(solution)/shard_map/all_gather | solution.py:23
  7.9 101.9 %all-gather.6.cloned.1.call-start = ((), (), s32[]{:S(2)}) async-start(), calls=%async_computation.7 | async-start | bytes 1290240 | tf_op jit(solution)/shard_map/all_gather | solution.py:34
  8.6 177.3 %reduce-scatter.6.cloned.1.call-start = ((), (), s32[]{:S(2)}) async-start(), calls=%async_computation.6 | async-start | bytes 774144 | tf_op jit(solution)/shard_map/reduce_scatter | solution.py:26
  87.5 3.0 copy-start.1
  90.4 183.9 %reduce-scatter.8.cloned.1.call-start = ((), (), s32[]{:S(2)}) async-start(), calls=%async_computation.8 | async-start | bytes 774144 | tf_op jit(solution)/shard_map/reduce_scatter | solution.py:37
  112.7 231.0 %copy-start.4 = (bf16[640,896]{1,0:T(8,128)(2,1)S(1)}, bf16[640,896]{1,0:T(8,128)(2,1)}, u32[]{:S(2)}) copy-start(bf16[640,896]{1,0:T(8,128)(2,1)} %all-gather.4.cloned.1.call-done) | copy-start | bytes 3440644
  112.8 230.9 %all-gather.8.cloned.1.call-start = ((), (), s32[]{:S(2)}) async-start(), calls=%async_computation.9 | async-start | bytes 1548288 | tf_op jit(solution)/shard_map/all_gather | solution.py:49
  276.1 105.5 %reduce-scatter.10.cloned.1.call-start = ((), (), s32[]{:S(2)}) async-start(), calls=%async_computation.10 | async-start | bytes 552960 | tf_op jit(solution)/shard_map/reduce_scatter | solution.py:75
  343.7 2.9 copy-start.3
  346.5 208.1 %reduce-scatter.12.cloned.1.call-start = ((), (), s32[]{:S(2)}) async-start(), calls=%async_computation.11 | async-start | bytes 1290240 | tf_op jit(solution)/shard_map/reduce_scatter | solution.py:66
  348.5 206.2 %reduce-scatter.14.cloned.1.call-start = ((), (), s32[]{:S(2)}) async-start(), calls=%async_computation.12 | async-start | bytes 1290240 | tf_op jit(solution)/shard_map/reduce_scatter | solution.py:57
  350.4 31.2 %copy-start = (bf16[48,640]{1,0:T(8,128)(2,1)S(1)}, bf16[48,640]{1,0:T(8,128)(2,1)}, u32[]{:S(2)}) copy-start(bf16[48,640]{1,0:T(8,128)(2,1)} %param.5) | copy-start | bytes 184324
  350.4 31.2 %copy-start.2 = (f32[640]{0:T(1024)S(1)}, f32[640]{0:T(1024)}, u32[]{:S(2)}) copy-start(f32[640]{0:T(1024)} %param.6) | copy-start | bytes 7684
Sparse Core Ops, SparseCore 0:
  10.1 43.7 all-gather.3
  56.0 38.5 all-gather.5
  99.1 86.8 reduce-scatter.5
  191.0 83.3 reduce-scatter.7
  277.4 66.2 all-gather.7
  346.6 34.8 reduce-scatter.9
  385.2 41.1 reduce-scatter.11
  430.0 39.8 reduce-scatter.13
